TPU v7x, 256 devices: a whole 4x4x8 slice. The times are simulated.
256 devices in a mesh: param: 32 (over y, x, core), walker: 8 (over z).
Axes of the slice: x: 4, y: 4, z: 8, core: 2. Of those that a mesh axis runs over, the one named last changes fastest.
Arguments:
- derivs: float32 [64, 4980736], P('walker', 'param'), may hold values from -1.7 to 1.7
- gradient: float32 [4980736], P('param'), may hold values from -0.01171875 to 0.01171875
Outputs:
- solution: float32 [4980736], P(('param', 'walker'))
All inputs are finite; a program needn't handle non-finite values.
Results may differ from a plain program's by a relative error of at most 0.0003.
Values sent between devices are 32-bit elements; how exact they have to be, the bound alone decides.
A program may use at most 64 MiB of HBM per device.

v0:
```python
import jax
import jax.numpy as jnp
from jax import lax
from jax.sharding import PartitionSpec as P

ITERS = 3
DAMPING = 0.001


def body(derivs, gradient):
    walkers = lax.axis_size("walker")
    rows_all = derivs.shape[0] * walkers
    share_len = gradient.shape[0] // walkers
    offset = lax.axis_index("walker") * share_len

    def own_share(vector):
        return lax.dynamic_slice_in_dim(vector, offset, share_len, 0)

    def local_view(vector):
        return own_share(vector)

    def squares(vector):
        return lax.psum(jnp.sum(vector * vector), ("param", "walker"))

    solution = jnp.zeros_like(gradient)
    residual = gradient
    direction = gradient
    norm_now = squares(local_view(gradient))
    for step_idx in range(ITERS):
        row_part = jnp.dot(derivs, direction, precision=lax.Precision.HIGHEST)
        row_vals = lax.psum(row_part, "param")
        back_vals = lax.psum(jnp.dot(row_vals, derivs, precision=lax.Precision.HIGHEST), "walker")
        image = back_vals / rows_all + DAMPING * direction
        advance_solution = solution
        advance_residual = residual
        dir_view = local_view(direction)
        img_view = local_view(image)
        curv_pq = lax.psum(jnp.sum(dir_view * img_view), ("param", "walker"))
        step_len = norm_now / curv_pq
        advance_residual = advance_residual - step_len * image
        norm_next = squares(local_view(advance_residual))
        advance_solution = advance_solution + step_len * direction
        solution, residual, norm_next = (advance_solution, advance_residual, norm_next)
        direction = residual + norm_next / norm_now * direction
        norm_now = norm_next
    return own_share(solution)


def solution(mesh):
    in_specs = (P("walker", "param"), P("param"))
    out_specs = P(("param", "walker"))
    return jax.shard_map(body, mesh=mesh, in_specs=in_specs, out_specs=out_specs, check_vma=False)
```

profile of v0, /device:TPU:1, one launch (start us, length us, event | category | flops | bytes accessed | tf_op | source)
XLA Modules:
  0.0 868.1 jit_solution(3013263644539260570)
XLA Ops:
  6.5 13.8 %convolution_bitcast_fusion.2 = f32[8]{0:T(128)S(1)} fusion(f32[8,155648]{1,0:T(8,128)} %param.2, f32[155648,1]{0,1:T(1,128)} %bitcast.30), kind=kOutput, calls=%fused_computation.2 | convolution fusion | flops 14942208 | bytes 5603360 | tf_op jit(solution)/shard_map/dot_general | solution.py:30
  20.3 65.4 %psum.85 = f32[8]{0:T(128)S(1)} all-reduce(f32[8]{0:T(128)S(1)} %convolution_bitcast_fusion.2), channel_id=1, replica_groups=mesh['param'=32,'walker'=8] {'param'}, use_global_device_ids=true, to_apply=%region_2.0 | all-reduce | flops 8 | bytes 64 | tf_op jit(solution)/shard_map/psum | solution.py:31
  85.7 7.7 fusion.7
  93.4 0.0 all-reduce.5.cloned.1.call-update
  93.5 0.0 all-reduce.7.cloned.1.call-start
  93.5 70.1 %all-reduce.5.cloned.1.call-done = f32[155648]{0:T(1024)} async-done(((f32[155648]{0:T(1024)}), f32[155648]{0:T(1024)}) %all-reduce.5.cloned.1.call-update) | async-done | bytes 622608 | tf_op jit(solution)/shard_map/psum | solution.py:32
  163.6 1.2 multiply_add_fusion.3
  164.8 0.6 multiply_reduce_fusion.3
  165.4 79.8 %all-reduce = (f32[]{:T(128)}, f32[]{:T(128)}) all-reduce(f32[]{:T(128)} %get-tuple-element.6, f32[]{:T(128)} %get-tuple-element.5), channel_id=1, replica_groups=mesh['param'=32,'walker'=8] {'param','walker'}, use_global_device_ids=true, to_apply=%region_1.0 | all-reduce | flops 2 | bytes 16 | tf_op jit(solution)/shard_map/psum | solution.py:23
  246.6 1.2 multiply_subtract_fusion.1
  247.8 0.6 multiply_reduce_fusion.2
  248.4 73.4 %psum.88 = f32[]{:T(128)} all-reduce(f32[]{:T(128)} %multiply_reduce_fusion.2), channel_id=1, replica_groups=mesh['param'=32,'walker'=8] {'param','walker'}, use_global_device_ids=true, to_apply=%region_7.0 | all-reduce | flops 1 | bytes 8 | tf_op jit(solution)/shard_map/psum | solution.py:23
  323.1 0.1 multiply_add_fusion.2
  323.2 12.7 %convolution_bitcast_fusion.1 = f32[8]{0:T(128)S(1)} fusion(f32[155648,1]{0,1:T(1,128)S(1)} %bitcast.31, f32[8,155648]{1,0:T(8,128)} %param.2), kind=kOutput, calls=%fused_computation.1 | convolution fusion | flops 14942208 | bytes 5603360 | tf_op jit(solution)/shard_map/dot_general | solution.py:30
  335.9 62.9 %psum.89 = f32[8]{0:T(128)S(1)} all-reduce(f32[8]{0:T(128)S(1)} %convolution_bitcast_fusion.1), channel_id=1, replica_groups=mesh['param'=32,'walker'=8] {'param'}, use_global_device_ids=true, to_apply=%region_8.0 | all-reduce | flops 8 | bytes 64 | tf_op jit(solution)/shard_map/psum | solution.py:31
  398.8 7.7 fusion.5
  406.5 0.0 all-reduce.9.cloned.1.call-start
  406.5 65.1 %all-reduce.7.cloned.1.call-done = f32[155648]{0:T(1024)} async-done(((f32[155648]{0:T(1024)}), f32[155648]{0:T(1024)}) %all-reduce.7.cloned.1.call-update) | async-done | bytes 622608 | tf_op jit(solution)/shard_map/psum | solution.py:32
  471.6 1.2 multiply_add_fusion.1
  472.8 0.7 multiply_reduce_fusion.1
  473.5 79.7 %psum.91 = f32[]{:T(128)} all-reduce(f32[]{:T(128)} %multiply_reduce_fusion.1), channel_id=1, replica_groups=mesh['param'=32,'walker'=8] {'param','walker'}, use_global_device_ids=true, to_apply=%region_11.0 | all-reduce | flops 1 | bytes 8 | tf_op jit(solution)/shard_map/psum | solution.py:38
  554.6 0.1 multiply_subtract_fusion
  554.7 0.6 multiply_reduce_fusion
  555.3 73.4 %psum.92 = f32[]{:T(128)} all-reduce(f32[]{:T(128)} %multiply_reduce_fusion), channel_id=1, replica_groups=mesh['param'=32,'walker'=8] {'param','walker'}, use_global_device_ids=true, to_apply=%region_13.0 | all-reduce | flops 1 | bytes 8 | tf_op jit(solution)/shard_map/psum | solution.py:23
  630.0 0.1 multiply_add_fusion
  630.1 12.7 %convolution_bitcast_fusion = f32[8]{0:T(128)S(1)} fusion(f32[155648,1]{0,1:T(1,128)S(1)} %bitcast.32, f32[8,155648]{1,0:T(8,128)} %param.2), kind=kOutput, calls=%fused_computation | convolution fusion | flops 14942208 | bytes 5603360 | tf_op jit(solution)/shard_map/dot_general | solution.py:30
  642.7 62.9 %psum.93 = f32[8]{0:T(128)S(1)} all-reduce(f32[8]{0:T(128)S(1)} %convolution_bitcast_fusion), channel_id=1, replica_groups=mesh['param'=32,'walker'=8] {'param'}, use_global_device_ids=true, to_apply=%region_14.0 | all-reduce | flops 8 | bytes 64 | tf_op jit(solution)/shard_map/psum | solution.py:31
  705.6 7.7 fusion.3
  713.4 65.1 %all-reduce.9.cloned.1.call-done = f32[155648]{0:T(1024)} async-done(((f32[155648]{0:T(1024)}), f32[155648]{0:T(1024)}) %all-reduce.9.cloned.1.call-update) | async-done | bytes 622608 | tf_op jit(solution)/shard_map/psum | solution.py:32
  778.4 1.5 fusion.2
  780.0 79.7 %psum.95 = f32[]{:T(128)} all-reduce(f32[]{:T(128)} %fusion.2), channel_id=1, replica_groups=mesh['param'=32,'walker'=8] {'param','walker'}, use_global_device_ids=true, to_apply=%region_17.0 | all-reduce | flops 1 | bytes 8 | tf_op jit(solution)/shard_map/psum | solution.py:38
  860.9 0.7 multiply_add_fusion.4
  (5 shorter events, 0.0 us)
Async XLA Ops:
  6.5 157.1 %all-reduce.5.cloned.1.call-start = ((), (), s32[]{:S(2)}) async-start(), calls=%async_computation | async-start | bytes 1245184 | tf_op jit(solution)/shard_map/psum | solution.py:32
  6.5 157.1 %copy-start = (f32[155648]{0:T(1024)S(1)}, f32[155648]{0:T(1024)}, u32[]{:S(2)}) copy-start(f32[155648]{0:T(1024)} %param.3) | copy-start | bytes 1867780
  93.5 378.2 %all-reduce.7.cloned.1.call-start = ((), (), s32[]{:S(2)}) async-start(), calls=%async_computation.1 | async-start | bytes 1245184 | tf_op jit(solution)/shard_map/psum | solution.py:32
  406.5 372.0 %all-reduce.9.cloned.1.call-start = ((), (), s32[]{:S(2)}) async-start(), calls=%async_computation.2 | async-start | bytes 1245184 | tf_op jit(solution)/shard_map/psum | solution.py:32
Sparse Core Ops, SparseCore 0:
  93.6 70.0 all-reduce.4
  406.6 64.9 all-reduce.6
  713.5 64.9 all-reduce.8
where the time goes:
time: 869 us; the launch traced here: 868 us
  blocking collectives  577 us (66%)
  waiting for transfers between devices  200 us (23%)
  matrix products  62.1 us (7%)
  between operations  19.8 us (2%)
    psum x3, blocking collectives, squares(): return lax.psum(jnp.sum(vector * vector), ('param', 'walker'))  227 us
    psum x3, waiting for transfers between devices, body(): lax.psum(jnp.dot(row_vals, derivs, precision=lax.Precision.HIGHEST), 'wal...  200 us
    psum x3, blocking collectives, body(): row_vals = lax.psum(row_part, 'param')  191 us
    psum x2, blocking collectives, body(): curv_pq = lax.psum(jnp.sum(dir_view * img_view), ('param', 'walker'))  159 us
    dot_general x3, matrix products, body(): row_part = jnp.dot(derivs, direction, precision=lax.Precision.HIGHEST)  39.1 us
    dot_general x3, matrix products, body(): jnp.dot(row_vals, derivs, precision=lax.Precision.HIGHEST)  23.1 us
  transfers between devices with their start and end apart: 3, of which 3 were waited for; matrix products, arithmetic and copies ran while one was open for 0% of the time, Pallas kernels for 0%

commit v1 on v0

--- a/solution.py
+++ b/solution.py
@@ -28,7 +28,11 @@
     norm_now = squares(local_view(gradient))
     for step_idx in range(ITERS):
         row_part = jnp.dot(derivs, direction, precision=lax.Precision.HIGHEST)
-        row_vals = lax.psum(row_part, "param")
+        row_vals = row_part
+        for hop in (1, 2, 4, 8, 16):
+            row_vals = row_vals + lax.ppermute(
+                row_vals, "param", [(dev, dev ^ hop) for dev in range(32)]
+            )
         back_vals = lax.psum(jnp.dot(row_vals, derivs, precision=lax.Precision.HIGHEST), "walker")
         image = back_vals / rows_all + DAMPING * direction
         advance_solution = solution

time: 869 us -> 743 us (0.86)
  blocking collectives: 577 us -> 386 us
  waiting for transfers between devices: 200 us -> 244 us
  starting transfers between devices: 0.09 us -> 17 us
    psum x3 -> x0, blocking collectives: 191 us -> none  [body(): row_vals = lax.psum(row_part, 'param')]
    ppermute x0 -> x15, waiting for transfers between devices: none -> 28.6 us  [body(): lax.ppermute(row_vals, 'param', [(dev, dev ^ hop) for dev in range(32)])]
    ppermute x0 -> x15, starting transfers between devices: none -> 16.9 us  [body(): lax.ppermute(row_vals, 'param', [(dev, dev ^ hop) for dev in range(32)])]
    psum x3, waiting for transfers between devices: 200 us -> 215 us  [body(): lax.psum(jnp.dot(row_vals, derivs, precision=lax.Precision.HIGHEST), 'wal...]
  transfers between devices with their start and end apart: 3 -> 18, of which waited for: 3 -> 18; matrix products, arithmetic and copies ran while one was open for 0% -> 0% of each run, Pallas kernels for 0% -> 0%
where the time goes in v1:
time: 743 us; the launch traced here: 735 us
  blocking collectives  386 us (52%)
  waiting for transfers between devices  244 us (33%)
  matrix products  59.7 us (8%)
  between operations  20 us (3%)
  starting transfers between devices  17 us (2%)
  other arithmetic  8.48 us (1%)
    psum x3, blocking collectives, squares(): return lax.psum(jnp.sum(vector * vector), ('param', 'walker'))  227 us
    psum x3, waiting for transfers between devices, body(): lax.psum(jnp.dot(row_vals, derivs, precision=lax.Precision.HIGHEST), 'wal...  215 us
    psum x2, blocking collectives, body(): curv_pq = lax.psum(jnp.sum(dir_view * img_view), ('param', 'walker'))  159 us
    dot_general x3, matrix products, body(): row_part = jnp.dot(derivs, direction, precision=lax.Precision.HIGHEST)  39.1 us
    ppermute x15, waiting for transfers between devices, body(): lax.ppermute(row_vals, 'param', [(dev, dev ^ hop) for dev in range(32)])  28.6 us
    dot_general x3, matrix products, body(): jnp.dot(row_vals, derivs, precision=lax.Precision.HIGHEST)  20.5 us
    ppermute x15, starting transfers between devices, body(): lax.ppermute(row_vals, 'param', [(dev, dev ^ hop) for dev in range(32)])  16.9 us
  transfers between devices with their start and end apart: 18, of which 18 were waited for; matrix products, arithmetic and copies ran while one was open for 0% of the time, Pallas kernels for 0%

profile of v1, /device:TPU:1, one launch (start us, length us, event | category | flops | bytes accessed | tf_op | source)
XLA Modules:
  0.0 734.9 jit_solution(3960659716172686963)
XLA Ops:
  6.5 13.8 %convolution_bitcast_fusion.2 = f32[8]{0:T(128)S(1)} fusion(f32[8,155648]{1,0:T(8,128)} %param.2, f32[155648,1]{0,1:T(1,128)} %bitcast.30), kind=kOutput, calls=%fused_computation.2 | convolution fusion | flops 14942208 | bytes 5603360 | tf_op jit(solution)/shard_map/dot_general | solution.py:30
  20.4 3.3 collective-permute-start
  24.5 2.4 collective-permute-done.1
  27.9 2.9 collective-permute-done.2
  30.8 2.4 collective-permute-done.3
  33.1 1.6 collective-permute-start.4
  34.8 2.7 collective-permute-done.4
  37.5 5.2 fusion.7
  42.7 74.8 %all-reduce.5.cloned.1.call-done = f32[155648]{0:T(1024)} async-done(((f32[155648]{0:T(1024)}), f32[155648]{0:T(1024)}) %all-reduce.5.cloned.1.call-update) | async-done | bytes 622608 | tf_op jit(solution)/shard_map/psum | solution.py:36
  119.3 79.8 %all-reduce = (f32[]{:T(128)}, f32[]{:T(128)}) all-reduce(f32[]{:T(128)} %get-tuple-element.6, f32[]{:T(128)} %get-tuple-element.5), channel_id=1, replica_groups=mesh['param'=32,'walker'=8] {'param','walker'}, use_global_device_ids=true, to_apply=%region_1.0 | all-reduce | flops 2 | bytes 16 | tf_op jit(solution)/shard_map/psum | solution.py:23
  202.3 73.4 %psum.66 = f32[]{:T(128)} all-reduce(f32[]{:T(128)} %multiply_reduce_fusion.2), channel_id=1, replica_groups=mesh['param'=32,'walker'=8] {'param','walker'}, use_global_device_ids=true, to_apply=%region_6.0 | all-reduce | flops 1 | bytes 8 | tf_op jit(solution)/shard_map/psum | solution.py:23
  277.1 12.7 %convolution_bitcast_fusion.1 = f32[8]{0:T(128)S(1)} fusion(f32[155648,1]{0,1:T(1,128)S(1)} %bitcast.31, f32[8,155648]{1,0:T(8,128)} %param.2), kind=kOutput, calls=%fused_computation.1 | convolution fusion | flops 14942208 | bytes 5603360 | tf_op jit(solution)/shard_map/dot_general | solution.py:30
  292.0 1.7 collective-permute-done.6
  293.7 1.7 collective-permute-start.7
  295.3 2.2 collective-permute-done.7
  298.3 1.7 collective-permute-done.8
  300.0 1.8 collective-permute-start.9
  301.8 2.2 collective-permute-done.9
  304.0 7.7 %fusion.5 = f32[1,155648]{1,0:T(1,128)} fusion(f32[8,155648]{1,0:T(8,128)} %param.2, f32[8]{0:T(128)S(1)} %add.107, f32[8]{0:T(128)S(1)} %collective-permute-done.9), kind=kOutput, calls=%fused_computation.21 | convolution fusion | flops 14942216 | bytes 5603392 | tf_op jit(solution)/shard_map/dot_general | solution.py:36
  311.8 70.1 %all-reduce.7.cloned.1.call-done = f32[155648]{0:T(1024)} async-done(((f32[155648]{0:T(1024)}), f32[155648]{0:T(1024)}) %all-reduce.7.cloned.1.call-update) | async-done | bytes 622608 | tf_op jit(solution)/shard_map/psum | solution.py:36
  383.7 79.7 %psum.68 = f32[]{:T(128)} all-reduce(f32[]{:T(128)} %multiply_reduce_fusion.1), channel_id=1, replica_groups=mesh['param'=32,'walker'=8] {'param','walker'}, use_global_device_ids=true, to_apply=%region_9.0 | all-reduce | flops 1 | bytes 8 | tf_op jit(solution)/shard_map/psum | solution.py:42
  465.5 73.4 %psum.69 = f32[]{:T(128)} all-reduce(f32[]{:T(128)} %multiply_reduce_fusion), channel_id=1, replica_groups=mesh['param'=32,'walker'=8] {'param','walker'}, use_global_device_ids=true, to_apply=%region_11.0 | all-reduce | flops 1 | bytes 8 | tf_op jit(solution)/shard_map/psum | solution.py:23
  540.3 12.7 %convolution_bitcast_fusion = f32[8]{0:T(128)S(1)} fusion(f32[155648,1]{0,1:T(1,128)S(1)} %bitcast.32, f32[8,155648]{1,0:T(8,128)} %param.2), kind=kOutput, calls=%fused_computation | convolution fusion | flops 14942208 | bytes 5603360 | tf_op jit(solution)/shard_map/dot_general | solution.py:30
  555.1 1.7 collective-permute-done.11
  556.8 1.6 collective-permute-start.12
  558.4 2.3 collective-permute-done.12
  561.6 1.7 collective-permute-done.13
  563.3 1.6 collective-permute-start.14
  564.9 2.3 collective-permute-done.14
  567.2 7.7 %fusion.3 = f32[1,155648]{1,0:T(1,128)} fusion(f32[8,155648]{1,0:T(8,128)} %param.2, f32[8]{0:T(128)S(1)} %add.115, f32[8]{0:T(128)S(1)} %collective-permute-done.14), kind=kOutput, calls=%fused_computation.19 | convolution fusion | flops 14942216 | bytes 5603392 | tf_op jit(solution)/shard_map/dot_general | solution.py:36
  574.9 70.1 %all-reduce.9.cloned.1.call-done = f32[155648]{0:T(1024)} async-done(((f32[155648]{0:T(1024)}), f32[155648]{0:T(1024)}) %all-reduce.9.cloned.1.call-update) | async-done | bytes 622608 | tf_op jit(solution)/shard_map/psum | solution.py:36
  646.5 79.7 %psum.71 = f32[]{:T(128)} all-reduce(f32[]{:T(128)} %fusion.2), channel_id=1, replica_groups=mesh['param'=32,'walker'=8] {'param','walker'}, use_global_device_ids=true, to_apply=%region_14.0 | all-reduce | flops 1 | bytes 8 | tf_op jit(solution)/shard_map/psum | solution.py:42
  (46 shorter events, 16.4 us)
Async XLA Ops:
  6.5 111.0 %all-reduce.5.cloned.1.call-start = ((), (), s32[]{:S(2)}) async-start(), calls=%async_computation | async-start | bytes 1245184 | tf_op jit(solution)/shard_map/psum | solution.py:36
  6.5 31.0 %copy-start = (f32[8,155648]{1,0:T(8,128)S(1)}, f32[8,155648]{1,0:T(8,128)}, u32[]{:S(2)}) copy-start(f32[8,155648]{1,0:T(8,128)} %param.2) | copy-start | bytes 14942212
  6.5 111.0 %copy-start.1 = (f32[155648]{0:T(1024)S(1)}, f32[155648]{0:T(1024)}, u32[]{:S(2)}) copy-start(f32[155648]{0:T(1024)} %param.3) | copy-start | bytes 1867780
  20.4 4.1 collective-permute-start
  24.5 2.4 collective-permute-start.1
  26.9 3.9 collective-permute-start.2
  30.8 2.4 collective-permute-start.3
  33.1 4.3 collective-permute-start.4
  42.7 339.2 %all-reduce.7.cloned.1.call-start = ((), (), s32[]{:S(2)}) async-start(), calls=%async_computation.1 | async-start | bytes 1245184 | tf_op jit(solution)/shard_map/psum | solution.py:36
  289.8 1.5 collective-permute-start.5
  291.3 2.4 collective-permute-start.6
  293.7 3.9 collective-permute-start.7
  297.6 2.4 collective-permute-start.8
  300.0 4.0 collective-permute-start.9
  311.7 333.3 %all-reduce.9.cloned.1.call-start = ((), (), s32[]{:S(2)}) async-start(), calls=%async_computation.2 | async-start | bytes 1245184 | tf_op jit(solution)/shard_map/psum | solution.py:36
  552.9 1.5 collective-permute-start.10
  554.4 2.4 collective-permute-start.11
  556.8 3.9 collective-permute-start.12
  560.7 2.6 collective-permute-start.13
  563.3 3.9 collective-permute-start.14
Sparse Core Ops, SparseCore 0:
  42.8 74.7 all-reduce.4
  311.8 69.9 all-reduce.6
  575.0 69.8 all-reduce.8
